TPU v7x, 128 devices: a whole 4x4x4 slice. The times are simulated.
128 devices in a mesh: ctx: 16 (over z, x), tp: 8 (over y, core).
Axes of the slice: x: 4, y: 4, z: 4, core: 2. Of those that a mesh axis runs over, the one named last changes fastest.
Arguments:
- projected: bfloat16 [3, 8192, 8192], P(None, 'ctx', 'tp'), may hold values from -6 to 6
- short_filter: float32 [3, 3, 8192], P(None, None, 'tp'), may hold values from -3.5 to 3.5
- long_filter: bfloat16 [128, 8192], P(None, 'tp'), may hold values from -0.5 to 0.5
- skip_gain: float32 [8192], P('tp'), may hold values from -3 to 3
- out_weight: bfloat16 [8192, 8192], P('tp', 'ctx'), may hold values from -0.0625 to 0.0625
- out_grad: bfloat16 [8192, 8192], P('ctx'), may hold values from -6 to 6
- left_source: int32 [16], replicated, may hold values from -1 to 15, as said below
Outputs:
- mixed: bfloat16 [8192, 8192], P(('ctx', 'tp'))
- grad_projected: bfloat16 [3, 8192, 8192], P(None, 'ctx', 'tp')
- grad_long: float32 [128, 8192], P(None, 'tp')
- grad_short: float32 [3, 3, 8192], P(None, None, 'tp')
Inputs may be any that keep to these rules, and one draw needn't show every extreme that they name: left_source[b] is -1 where block b begins a contig, else another block; no block is named by two blocks, and following left_source from any block ends at -1 without repeating a block.
All inputs are finite; a program needn't handle non-finite values.
Results may differ from a plain program's by a relative error of at most 0.015.
Values may be sent and summed in bfloat16 or wider, within the bound.
No kernel may reach another device: no remote copies, remote signals or barrier semaphores. Data moves between devices by JAX's collectives and lax.ppermute only.
A program may use at most 128 MiB of HBM per device.

v0:
```python
import math
import jax
import jax.numpy as jnp
from jax import lax
from jax.sharding import PartitionSpec as P

edge_depth = 8


def short_forward(extended, tap_weights, out_rows):
    summed = jnp.zeros((extended.shape[0], out_rows, extended.shape[2]), jnp.float32)
    for shift in range(tap_weights.shape[1]):
        piece = extended[:, edge_depth - shift : edge_depth - shift + out_rows].astype(jnp.float32)
        summed = summed + tap_weights[:, shift][:, None, :] * piece
    return summed


def depthwise(signal, kernel):
    channels = signal.shape[1]
    result = lax.conv_general_dilated(
        signal[None],
        kernel[:, None, :],
        (1,),
        "VALID",
        dimension_numbers=("NWC", "WIO", "NWC"),
        feature_group_count=channels,
        preferred_element_type=jnp.float32,
    )
    return result[0]


def causal_conv(extended, flipped_taps):
    return depthwise(extended[1:], flipped_taps)


def lag_sums(grad_conv, extended):
    return jnp.flip(depthwise(extended[1:], grad_conv), 0)


def select_slot(stacked, slot, live):
    picked = lax.dynamic_index_in_dim(stacked, slot, 0, keepdims=False)
    return jnp.where(live, picked, jnp.zeros_like(picked))


def on_device(projected, short_filter, long_filter, skip_gain, out_weight, out_grad, left_source):
    rows_here = projected.shape[1]
    filt_len = long_filter.shape[0]
    ctx_count = lax.axis_size("ctx")
    my_index = lax.axis_index("ctx")
    positions = jnp.arange(ctx_count, dtype=jnp.int32)
    source_raw = left_source[my_index]
    has_left = source_raw >= 0
    source = jnp.maximum(source_raw, 0)
    is_reader = left_source == my_index
    has_right = jnp.any(is_reader)
    reader = jnp.sum(jnp.where(is_reader, positions, 0))
    flipped_taps = jnp.flip(long_filter, 0)
    skip_row = skip_gain[None, :]
    act_rest = short_forward(projected, short_filter, rows_here - edge_depth)
    mixin_rest = (act_rest[1] * act_rest[2]).astype(jnp.bfloat16)
    raw_tail = projected[:, rows_here - edge_depth :]
    mixin_tail = mixin_rest[mixin_rest.shape[0] - filt_len :]
    slot_mark = ((positions == reader) & has_right).astype(jnp.bfloat16)
    sent_raw = slot_mark[:, None, None, None] * raw_tail[None]
    sent_mixin = slot_mark[:, None, None] * mixin_tail[None]
    got_raw, got_mixin = (
        lax.all_to_all(sent_raw, "ctx", split_axis=0, concat_axis=0, tiled=True),
        lax.all_to_all(sent_mixin, "ctx", split_axis=0, concat_axis=0, tiled=True),
    )
    left_raw = select_slot(got_raw, source, has_left)
    left_mixin = select_slot(got_mixin, source, has_left)
    streams_ext = jnp.concatenate([left_raw, projected], 1)
    act_head = short_forward(streams_ext[:, : 2 * edge_depth], short_filter, edge_depth)
    act = jnp.concatenate([act_head, act_rest], 1)
    mixin_head = (act_head[1] * act_head[2]).astype(jnp.bfloat16)
    mixin = jnp.concatenate([mixin_head, mixin_rest], 0)
    mixin_ext = jnp.concatenate([left_mixin, mixin], 0)
    conv = causal_conv(mixin_ext, flipped_taps)
    conv = conv + skip_row * mixin.astype(jnp.float32)
    gated = (act[0] * conv).astype(jnp.bfloat16)
    full_weight = lax.all_gather(out_weight, "ctx", axis=1, tiled=True)
    share_rows = rows_here // lax.axis_size("tp")
    gated_rows = lax.slice_in_dim(gated, 0, lax.axis_size("tp") * share_rows, axis=0)
    mixed = lax.psum_scatter(
        jnp.dot(gated_rows, full_weight, preferred_element_type=jnp.float32).astype(jnp.bfloat16),
        "tp",
        scatter_dimension=0,
        tiled=True,
    )
    back_grad = lax.dot_general(
        out_grad, full_weight, (((1,), (1,)), ((), ())), preferred_element_type=jnp.float32
    )
    grad_conv = (back_grad * act[0]).astype(jnp.bfloat16)
    grad_gate = back_grad * conv
    flipped = jnp.flip(grad_conv, 0)
    back_mark = ((positions == source) & has_left).astype(jnp.bfloat16)
    sent_head = back_mark[:, None, None] * grad_conv[None, :filt_len]
    got_head = lax.all_to_all(sent_head, "ctx", split_axis=0, concat_axis=0, tiled=True)
    right_head = select_slot(got_head, reader, has_right)
    flipped_ext = jnp.concatenate([jnp.flip(right_head, 0), flipped], 0)
    flipped_conv = causal_conv(flipped_ext, flipped_taps)
    grad_wide = grad_conv.astype(jnp.float32)
    grad_mixin = jnp.flip(flipped_conv, 0) + skip_row * grad_wide
    grad_act = jnp.stack([grad_gate, grad_mixin * act[2], grad_mixin * act[1]])
    wide_mark = back_mark.astype(jnp.float32)
    sent_rows = wide_mark[:, None, None, None] * grad_act[None, :, :edge_depth]
    got_rows = lax.all_to_all(
        sent_rows.astype(jnp.bfloat16), "ctx", split_axis=0, concat_axis=0, tiled=True
    ).astype(sent_rows.dtype)
    right_rows = select_slot(got_rows, reader, has_right)
    grad_act_ext = jnp.concatenate([grad_act, right_rows], 1)
    grad_streams = jnp.zeros(grad_act.shape, jnp.float32)
    for shift in range(short_filter.shape[1]):
        grad_streams = (
            grad_streams
            + short_filter[:, shift][:, None, :] * grad_act_ext[:, shift : shift + rows_here]
        )
    short_terms = jnp.stack(
        [
            jnp.sum(
                grad_act
                * streams_ext[:, edge_depth - shift : edge_depth - shift + rows_here].astype(
                    jnp.float32
                ),
                axis=1,
            )
            for shift in range(short_filter.shape[1])
        ],
        axis=1,
    )
    long_terms = lag_sums(grad_conv, mixin_ext)
    long_total, short_total = (
        lax.psum(long_terms.astype(jnp.bfloat16), "ctx").astype(jnp.float32),
        lax.psum(short_terms.astype(jnp.bfloat16), "ctx").astype(jnp.float32),
    )
    grad_scale = 1.0 / math.sqrt(rows_here * ctx_count)
    return (
        mixed,
        grad_streams.astype(jnp.bfloat16),
        long_total * grad_scale,
        short_total * grad_scale,
    )


def solution(mesh):
    placed = (
        P(None, "ctx", "tp"),
        P(None, None, "tp"),
        P(None, "tp"),
        P("tp"),
        P("tp", "ctx"),
        P("ctx", None),
        P(),
    )
    return jax.shard_map(
        on_device,
        mesh=mesh,
        in_specs=placed,
        out_specs=(
            P(("ctx", "tp"), None),
            P(None, "ctx", "tp"),
            P(None, "tp"),
            P(None, None, "tp"),
        ),
        check_vma=False,
    )
```

profile of v0, /device:TPU:24, one launch (start us, length us, event | category | flops | bytes accessed | tf_op | source)
XLA Modules:
  0.0 475.2 jit_solution(3345166502420664161)
XLA Ops:
  7.2 0.7 all-gather.2.cloned.1.call-update
  7.9 0.9 slice.97
  8.9 1.3 compare_reduce_fusion
  10.2 1.3 fusion.28
  11.5 1.2 and_convert_fusion.1
  12.8 1.0 broadcast_multiply_fusion.2
  13.8 7.9 %all-to-all-start = ((bf16[16,3,8,1024]{3,2,1,0:T(8,128)(2,1)}), bf16[16,3,8,1024]{3,2,1,0:T(8,128)(2,1)}, u32[]{:S(2)}, u32[]{:S(2)}) async-start(bf16[16,3,8,1024]{3,2,1,0:T(8,128)(2,1)} %broadcast_multiply_fusion.2), calls=%async_computation | async-start | bytes 1572864 | tf_op jit(solution)/shard_map/all_to_all | solution.py:67
  21.8 2.3 multiply_add_fusion
  24.1 2.7 copy-done.2
  27.1 2.4 broadcast_multiply_fusion.1
  29.4 12.3 %all-to-all-done = bf16[16,3,8,1024]{3,2,1,0:T(8,128)(2,1)} async-done(((bf16[16,3,8,1024]{3,2,1,0:T(8,128)(2,1)}), bf16[16,3,8,1024]{3,2,1,0:T(8,128)(2,1)}, u32[]{:S(2)}, u32[]{:S(2)}) %all-to-all-start) | async-done | bytes 786464 | tf_op jit(solution)/shard_map/all_to_all | solution.py:67
  41.7 4.5 all-to-all-start.1
  46.3 0.6 dynamic_slice.18
  48.2 2.8 rev.19
  51.0 3.5 fusion.36
  54.5 0.8 select_bitcast_fusion.3
  55.4 0.5 copy-done.9
  56.0 66.2 %all-to-all-done.1 = bf16[16,128,1024]{2,1,0:T(8,128)(2,1)} async-done(((bf16[16,128,1024]{2,1,0:T(8,128)(2,1)}), bf16[16,128,1024]{2,1,0:T(8,128)(2,1)}, u32[]{:S(2)}, u32[]{:S(2)}) %all-to-all-start.1) | async-done | bytes 4194336 | tf_op jit(solution)/shard_map/all_to_all | solution.py:68
  122.2 1.0 select_bitcast_fusion.1
  123.1 1.6 fusion.22
  124.7 1.1 copy-done.8
  125.8 32.3 %fusion.19 = f32[1,512,1024]{2,0,1:T(1,128)} fusion(bf16[1,639,1024]{2,1,0:T(8,128)(2,1)S(1)} %fusion.22, bf16[128,1,1024]{2,0,1:T(8,128)(2,1)S(1)} %bitcast.82), kind=kOutput, calls=%fused_computation.45 | convolution fusion | flops 134217728 | bytes 3667968 | tf_op jit(solution)/shard_map/conv_general_dilated | solution.py:20
  158.1 23.1 %all-gather.2.cloned.1.call-done = bf16[1024,8192]{1,0:T(8,128)(2,1)} async-done(((bf16[1024,512]{1,0:T(8,128)(2,1)}), bf16[1024,8192]{1,0:T(8,128)(2,1)}) %all-gather.2.cloned.1.call-update) | async-done | bytes 16777232 | tf_op jit(solution)/shard_map/all_gather | solution.py:81
  181.2 16.8 %multiply_bitcast_fusion = (f32[1,512,1024]{2,1,0:T(8,128)}, bf16[512,1024]{1,0:T(8,128)(2,1)S(1)}) fusion(f32[1,512,1024]{2,0,1:T(1,128)} %fusion.19, f32[1024]{0:T(1024)S(1)} %copy-done.20, bf16[504,1024]{1,0:T(8,128)(2,1)S(1)} %copy-done.7, bf16[8,1024]{1,0:T(8,128)(2,1)S(1)} %fusion.27, f32[3,504,1024]{2,1,0:T(8,128)} %copy-done.2, ...), kind=kOutput, calls=%fused_computation.39 | convolution fusion | flops 8595177472 | bytes 37752832 | tf_op jit(solution)/shard_map/dot_general | solution.py:90
  198.0 28.3 %fusion.15 = bf16[1,128,1024]{2,0,1:T(2,128)(2,1)S(1)} fusion(bf16[512,1,1024]{2,0,1:T(8,128)(2,1)S(1)} %bitcast.80, bf16[1,639,1024]{2,1,0:T(8,128)(2,1)} %copy-done.8), kind=kOutput, calls=%fused_computation.34 | convolution fusion | flops 134217728 | bytes 2619392 | tf_op jit(solution)/shard_map/conv_general_dilated | solution.py:20
  226.4 2.6 rev.23
  229.0 17.8 %convolution_convert_fusion = bf16[512,8192]{1,0:T(8,128)(2,1)} fusion(bf16[1024,8192]{1,0:T(8,128)(2,1)} %all-gather.2.cloned.1.call-done, f32[1,512,1024]{2,0,1:T(1,128)} %fusion.19, f32[1024]{0:T(1024)S(1)} %copy-done.20, bf16[504,1024]{1,0:T(8,128)(2,1)S(1)} %copy-done.7, bf16[8,1024]{1,0:T(8,128)(2,1)S(1)} %fusion.27, f32[3,504,1024]{2,1,0:T(8,128)} %copy-done.2, ...), kind=kOutput, calls=%fused_computation | convolution fusion | flops 8598847488 | bytes 34607104 | tf_op jit(solution)/shard_map/dot_general | solution.py:85
  246.9 2.4 broadcast_multiply_fusion
  249.3 7.8 %all-to-all-start.2 = ((bf16[16,128,1024]{2,1,0:T(8,128)(2,1)}), bf16[16,128,1024]{2,1,0:T(8,128)(2,1)}, u32[]{:S(2)}, u32[]{:S(2)}) async-start(bf16[16,128,1024]{2,1,0:T(8,128)(2,1)} %broadcast_multiply_fusion), calls=%async_computation.3 | async-start | bytes 8388608 | tf_op jit(solution)/shard_map/all_to_all | solution.py:98
  258.9 1.3 rev.21
  260.3 58.0 %all-to-all-done.2 = bf16[16,128,1024]{2,1,0:T(8,128)(2,1)} async-done(((bf16[16,128,1024]{2,1,0:T(8,128)(2,1)}), bf16[16,128,1024]{2,1,0:T(8,128)(2,1)}, u32[]{:S(2)}, u32[]{:S(2)}) %all-to-all-start.2) | async-done | bytes 4194336 | tf_op jit(solution)/shard_map/all_to_all | solution.py:98
  318.2 1.6 select_bitcast_fusion
  320.5 31.7 %fusion.4 = f32[1,512,1024]{2,0,1:T(1,128)S(1)} fusion(bf16[1,639,1024]{2,1,0:T(8,128)(2,1)S(1)} %fusion.21, bf16[128,1,1024]{2,0,1:T(8,128)(2,1)S(1)} %bitcast.83), kind=kOutput, calls=%fused_computation.20 | convolution fusion | flops 134217728 | bytes 3667968 | tf_op jit(solution)/shard_map/conv_general_dilated | solution.py:20
  352.7 10.3 %rev.22 = f32[512,1024]{1,0:T(8,128)} reverse(f32[512,1024]{1,0:T(8,128)S(1)} %bitcast.79), dimensions={0} | reverse | bytes 4194304 | tf_op jit(solution)/shard_map/jit(_flip)/rev | solution.py:103
  363.0 3.9 fusion.9
  367.0 0.9 pad_maximum_fusion.1
  367.9 0.7 copy-done.3
  368.7 1.1 multiply_convert_fusion.2
  369.8 4.0 all-to-all-start.3
  373.8 1.8 convert_multiply_fusion
  375.6 10.8 %all-to-all-done.3 = bf16[16,3,8,1024]{3,2,1,0:T(8,128)(2,1)S(1)} async-done(((bf16[16,3,8,1024]{3,2,1,0:T(8,128)(2,1)}), bf16[16,3,8,1024]{3,2,1,0:T(8,128)(2,1)S(1)}, u32[]{:S(2)}, u32[]{:S(2)}) %all-to-all-start.3) | async-done | bytes 786464 | tf_op jit(solution)/shard_map/all_to_all | solution.py:107
  386.4 0.6 select_bitcast_fusion.2
  387.1 2.8 pad_maximum_fusion
  390.4 0.7 copy-done.4
  391.1 0.7 copy-done.6
  391.8 5.6 %multiply_reduce_fusion.1 = (bf16[3,1024]{1,0:T(4,128)(2,1)S(1)}, bf16[3,1024]{1,0:T(4,128)(2,1)S(1)}, bf16[3,1024]{1,0:T(4,128)(2,1)S(1)}, bf16[3,512,1024]{2,1,0:T(8,128)(2,1)}) fusion(bf16[3,8,1024]{2,1,0:T(8,128)(2,1)S(1)} %copy-done.10, bf16[3,512,1024]{2,1,0:T(8,128)(2,1)S(1)} %copy-done.1, f32[1,512,1024]{2,1,0:T(8,128)S(1)} %copy-done.4, ...), kind=kLoop, calls=%fused_computation.11 | loop fusion | flops 36166656 | bytes 25270272 | tf_op jit(solution)/shard_map/reduce_sum | solution.py:120
  397.4 70.6 %psum.15 = bf16[3,3,1024]{2,0,1:T(4,128)(2,1)S(1)} all-reduce(bf16[3,3,1024]{2,0,1:T(4,128)(2,1)S(1)} %pad_maximum_fusion.9), channel_id=1, replica_groups=mesh['ctx'=16,'tp'=8] {'ctx'}, use_global_device_ids=true, to_apply=%region_7.8 | all-reduce | flops 9216 | bytes 36864 | tf_op jit(solution)/shard_map/psum | solution.py:134
  468.0 0.6 copy.21
  (61 shorter events, 2.4 us)
Async XLA Ops:
  7.2 14.7 %copy-start = (bf16[3,512,1024]{2,1,0:T(8,128)(2,1)S(1)}, bf16[3,512,1024]{2,1,0:T(8,128)(2,1)}, u32[]{:S(2)}) copy-start(bf16[3,512,1024]{2,1,0:T(8,128)(2,1)} %param.7) | copy-start | bytes 9437188
  7.2 14.5 %copy-start.19 = (f32[3,3,1024]{2,1,0:T(4,128)S(1)}, f32[3,3,1024]{2,1,0:T(4,128)}, u32[]{:S(2)}) copy-start(f32[3,3,1024]{2,1,0:T(4,128)} %param.8) | copy-start | bytes 110596
  7.2 174.1 %all-gather.2.cloned.1.call-start = ((), (), s32[]{:S(2)}) async-start(), calls=%async_computation.5 | async-start | bytes 17825792 | tf_op jit(solution)/shard_map/all_gather | solution.py:81
  13.8 28.0 %all-to-all-start = ((bf16[16,3,8,1024]{3,2,1,0:T(8,128)(2,1)}), bf16[16,3,8,1024]{3,2,1,0:T(8,128)(2,1)}, u32[]{:S(2)}, u32[]{:S(2)}) async-start(bf16[16,3,8,1024]{3,2,1,0:T(8,128)(2,1)} %broadcast_multiply_fusion.2), calls=%async_computation | async-start | bytes 1572864 | tf_op jit(solution)/shard_map/all_to_all | solution.py:67
  21.8 33.6 %copy-start.13 = (f32[3,1,1024]{2,0,1:T(4,128)}, f32[3,1,1024]{2,0,1:T(4,128)S(1)}, u32[]{:S(2)}) copy-start(f32[3,1,1024]{2,0,1:T(4,128)S(1)} %copy.53) | copy-start | bytes 36868
  21.8 33.5 %copy-start.15 = (f32[3,1024]{1,0:T(4,128)}, f32[3,1024]{1,0:T(4,128)S(1)}, u32[]{:S(2)}) copy-start(f32[3,1024]{1,0:T(4,128)S(1)} %get-tuple-element.21) | copy-start | bytes 36868
  21.8 33.5 %copy-start.17 = (f32[3,1024]{1,0:T(4,128)}, f32[3,1024]{1,0:T(4,128)S(1)}, u32[]{:S(2)}) copy-start(f32[3,1024]{1,0:T(4,128)S(1)} %get-tuple-element.22) | copy-start | bytes 36868
  24.1 2.7 copy-start.2
  29.4 16.9 %copy-start.21 = (s32[16]{0:T(128)S(1)}, s32[16]{0:T(128)}, u32[]{:S(2)}) copy-start(s32[16]{0:T(128)} %param.13) | copy-start | bytes 196
  29.4 18.8 %copy-start.11 = (bf16[128,1024]{1,0:T(8,128)(2,1)S(1)}, bf16[128,1024]{1,0:T(8,128)(2,1)}, u32[]{:S(2)}) copy-start(bf16[128,1024]{1,0:T(8,128)(2,1)} %param.9) | copy-start | bytes 786436
  41.7 80.4 %all-to-all-start.1 = ((bf16[16,128,1024]{2,1,0:T(8,128)(2,1)}), bf16[16,128,1024]{2,1,0:T(8,128)(2,1)}, u32[]{:S(2)}, u32[]{:S(2)}) async-start(bf16[16,128,1024]{2,1,0:T(8,128)(2,1)} %broadcast_multiply_fusion.1), calls=%async_computation.1 | async-start | bytes 8388608 | tf_op jit(solution)/shard_map/all_to_all | solution.py:68
  46.3 327.5 %all-reduce.2.cloned.1.call-start = ((), (), s32[]{:S(2)}) async-start(), calls=%async_computation.7 | async-start | bytes 524288 | tf_op jit(solution)/shard_map/psum | solution.py:133
  55.4 0.6 copy-start.9
  55.4 70.4 %copy-start.12 = (bf16[128,1024]{1,0:T(8,128)(2,1)S(1)}, bf16[128,1024]{1,0:T(8,128)(2,1)}, u32[]{:S(2)}) copy-start(bf16[128,1024]{1,0:T(8,128)(2,1)} %rev.19) | copy-start | bytes 786436
  124.7 1.1 copy-start.8
  125.8 55.4 %copy-start.7 = (bf16[504,1024]{1,0:T(8,128)(2,1)S(1)}, bf16[504,1024]{1,0:T(8,128)(2,1)}, u32[]{:S(2)}) copy-start(bf16[504,1024]{1,0:T(8,128)(2,1)} %fusion.36) | copy-start | bytes 3096580
  125.8 55.4 %copy-start.20 = (f32[1024]{0:T(1024)S(1)}, f32[1024]{0:T(1024)}, u32[]{:S(2)}) copy-start(f32[1024]{0:T(1024)} %param.10) | copy-start | bytes 12292
  229.0 239.7 %reduce-scatter.2.cloned.1.call-start = ((), (), s32[]{:S(2)}) async-start(), calls=%async_computation.6 | async-start | bytes 9437184 | tf_op jit(solution)/shard_map/reduce_scatter | solution.py:84
  249.3 69.0 %all-to-all-start.2 = ((bf16[16,128,1024]{2,1,0:T(8,128)(2,1)}), bf16[16,128,1024]{2,1,0:T(8,128)(2,1)}, u32[]{:S(2)}, u32[]{:S(2)}) async-start(bf16[16,128,1024]{2,1,0:T(8,128)(2,1)} %broadcast_multiply_fusion), calls=%async_computation.3 | async-start | bytes 8388608 | tf_op jit(solution)/shard_map/all_to_all | solution.py:98
  363.0 4.0 copy-start.5
  367.0 1.7 copy-start.3
  369.8 16.6 %all-to-all-start.3 = ((bf16[16,3,8,1024]{3,2,1,0:T(8,128)(2,1)}), bf16[16,3,8,1024]{3,2,1,0:T(8,128)(2,1)S(1)}, u32[]{:S(2)}, u32[]{:S(2)}) async-start(bf16[16,3,8,1024]{3,2,1,0:T(8,128)(2,1)} %multiply_convert_fusion.2), calls=%async_computation.4 | async-start | bytes 1572864 | tf_op jit(solution)/shard_map/all_to_all | solution.py:107
  387.1 3.3 copy-start.1
  387.1 4.0 copy-start.4
  387.1 4.7 copy-start.6
  387.1 4.6 copy-start.10
  387.1 4.6 copy-start.14
  387.1 4.6 copy-start.16
  387.1 4.6 copy-start.18
Sparse Core Ops, SparseCore 0:
  10.1 171.0 all-gather.1
  229.1 118.2 all-reduce.1
  350.4 49.8 reduce-scatter.1
where the time goes:
time: 476 us; the launch traced here: 475 us
  waiting for transfers between devices  171 us (36%)
  matrix products  127 us (27%)
  blocking collectives  70.6 us (15%)
  other arithmetic  37.8 us (8%)
  local copies, waits for them, and re-layouts  27 us (6%)
  starting transfers between devices  24.4 us (5%)
  between operations  17.3 us (4%)
    conv_general_dilated x3, matrix products, depthwise(): lax.conv_general_dilated(signal[None], kernel[:, None, :], (1,), 'VALID',...  92.3 us
    psum x1, blocking collectives, on_device(): lax.psum(short_terms.astype(jnp.bfloat16), 'ctx').astype(jnp.float32)  70.6 us
    all_to_all x1, waiting for transfers between devices, on_device(): lax.all_to_all(sent_mixin, 'ctx', split_axis=0, concat_axis=0, tiled=True)  66.2 us
    all_to_all x1, waiting for transfers between devices, on_device(): lax.all_to_all(sent_head, 'ctx', split_axis=0, concat_axis=0, tiled=True)  58 us
    all_gather x1, waiting for transfers between devices, on_device(): full_weight = lax.all_gather(out_weight, 'ctx', axis=1, tiled=True)  23.1 us
    dot_general x1, matrix products, on_device(): jnp.dot(gated_rows, full_weight, preferred_element_type=jnp.float32)  17.8 us
    dot_general x1, matrix products, on_device(): lax.dot_general(out_grad, full_weight, (((1,), (1,)), ((), ())), preferre...  16.8 us
    all_to_all x1, waiting for transfers between devices, on_device(): lax.all_to_all(sent_raw, 'ctx', split_axis=0, concat_axis=0, tiled=True)  12.3 us
  transfers between devices with their start and end apart: 7, of which 5 were waited for; matrix products, arithmetic and copies ran while one was open for 29% of the time, Pallas kernels for 0%

commit v1 on v0

--- a/solution.py
+++ b/solution.py
@@ -131,7 +131,9 @@
     long_terms = lag_sums(grad_conv, mixin_ext)
     long_total, short_total = (
         lax.psum(long_terms.astype(jnp.bfloat16), "ctx").astype(jnp.float32),
-        lax.psum(short_terms.astype(jnp.bfloat16), "ctx").astype(jnp.float32),
+        jnp.sum(lax.all_gather(short_terms.astype(jnp.bfloat16), "ctx"), axis=0).astype(
+            jnp.float32
+        ),
     )
     grad_scale = 1.0 / math.sqrt(rows_here * ctx_count)
     return (

time: 476 us -> 427 us (0.90)
  blocking collectives: 70.6 us -> 21.6 us
    psum x1 -> x0, blocking collectives: 70.6 us -> none  [on_device(): lax.psum(short_terms.astype(jnp.bfloat16), 'ctx').astype(jnp.float32)]
    all_gather x0 -> x1, blocking collectives: none -> 21.6 us  [on_device(): lax.all_gather(short_terms.astype(jnp.bfloat16), 'ctx')]
  transfers between devices with their start and end apart: 7 -> 7, of which waited for: 5 -> 5; matrix products, arithmetic and copies ran while one was open for 29% -> 32% of each run, Pallas kernels for 0% -> 0%
where the time goes in v1:
time: 427 us; the launch traced here: 426 us
  waiting for transfers between devices  171 us (40%)
  matrix products  127 us (30%)
  other arithmetic  38.6 us (9%)
  local copies, waits for them, and re-layouts  26.4 us (6%)
  starting transfers between devices  24.4 us (6%)
  blocking collectives  21.6 us (5%)
  between operations  17.4 us (4%)
    conv_general_dilated x3, matrix products, depthwise(): lax.conv_general_dilated(signal[None], kernel[:, None, :], (1,), 'VALID',...  92.3 us
    all_to_all x1, waiting for transfers between devices, on_device(): lax.all_to_all(sent_mixin, 'ctx', split_axis=0, concat_axis=0, tiled=True)  66.2 us
    all_to_all x1, waiting for transfers between devices, on_device(): lax.all_to_all(sent_head, 'ctx', split_axis=0, concat_axis=0, tiled=True)  58 us
    all_gather x1, waiting for transfers between devices, on_device(): full_weight = lax.all_gather(out_weight, 'ctx', axis=1, tiled=True)  23.1 us
    all_gather x1, blocking collectives, on_device(): lax.all_gather(short_terms.astype(jnp.bfloat16), 'ctx')  21.6 us
    dot_general x1, matrix products, on_device(): jnp.dot(gated_rows, full_weight, preferred_element_type=jnp.float32)  17.8 us
    dot_general x1, matrix products, on_device(): lax.dot_general(out_grad, full_weight, (((1,), (1,)), ((), ())), preferre...  16.8 us
    all_to_all x1, waiting for transfers between devices, on_device(): lax.all_to_all(sent_raw, 'ctx', split_axis=0, concat_axis=0, tiled=True)  12.3 us
  transfers between devices with their start and end apart: 7, of which 5 were waited for; matrix products, arithmetic and copies ran while one was open for 32% of the time, Pallas kernels for 0%

profile of v1, /device:TPU:24, one launch (start us, length us, event | category | flops | bytes accessed | tf_op | source)
XLA Modules:
  0.0 426.3 jit_solution(6432763313315607577)
XLA Ops:
  7.2 0.7 all-gather.2.cloned.1.call-update
  7.9 0.9 slice.97
  8.9 1.3 compare_reduce_fusion
  10.2 1.3 fusion.28
  11.5 1.2 and_convert_fusion.1
  12.8 1.0 broadcast_multiply_fusion.2
  13.8 7.9 %all-to-all-start = ((bf16[16,3,8,1024]{3,2,1,0:T(8,128)(2,1)}), bf16[16,3,8,1024]{3,2,1,0:T(8,128)(2,1)}, u32[]{:S(2)}, u32[]{:S(2)}) async-start(bf16[16,3,8,1024]{3,2,1,0:T(8,128)(2,1)} %broadcast_multiply_fusion.2), calls=%async_computation | async-start | bytes 1572864 | tf_op jit(solution)/shard_map/all_to_all | solution.py:67
  21.8 2.3 multiply_add_fusion
  24.1 2.7 copy-done.2
  27.1 2.4 broadcast_multiply_fusion.1
  29.4 12.3 %all-to-all-done = bf16[16,3,8,1024]{3,2,1,0:T(8,128)(2,1)} async-done(((bf16[16,3,8,1024]{3,2,1,0:T(8,128)(2,1)}), bf16[16,3,8,1024]{3,2,1,0:T(8,128)(2,1)}, u32[]{:S(2)}, u32[]{:S(2)}) %all-to-all-start) | async-done | bytes 786464 | tf_op jit(solution)/shard_map/all_to_all | solution.py:67
  41.7 4.5 %all-to-all-start.1 = ((bf16[16,128,1024]{2,1,0:T(8,128)(2,1)}), bf16[16,128,1024]{2,1,0:T(8,128)(2,1)}, u32[]{:S(2)}, u32[]{:S(2)}) async-start(bf16[16,128,1024]{2,1,0:T(8,128)(2,1)} %broadcast_multiply_fusion.1), calls=%async_computation.1 | async-start | bytes 8388608 | tf_op jit(solution)/shard_map/all_to_all | solution.py:68
  46.3 0.6 dynamic_slice.18
  48.2 2.8 rev.19
  51.0 3.5 fusion.36
  54.5 0.8 select_bitcast_fusion.3
  55.4 0.5 copy-done.9
  56.0 66.2 %all-to-all-done.1 = bf16[16,128,1024]{2,1,0:T(8,128)(2,1)} async-done(((bf16[16,128,1024]{2,1,0:T(8,128)(2,1)}), bf16[16,128,1024]{2,1,0:T(8,128)(2,1)}, u32[]{:S(2)}, u32[]{:S(2)}) %all-to-all-start.1) | async-done | bytes 4194336 | tf_op jit(solution)/shard_map/all_to_all | solution.py:68
  122.2 1.0 select_bitcast_fusion.1
  123.1 1.6 fusion.22
  124.7 1.1 copy-done.8
  125.8 32.3 %fusion.19 = f32[1,512,1024]{2,0,1:T(1,128)} fusion(bf16[1,639,1024]{2,1,0:T(8,128)(2,1)S(1)} %fusion.22, bf16[128,1,1024]{2,0,1:T(8,128)(2,1)S(1)} %bitcast.82), kind=kOutput, calls=%fused_computation.45 | convolution fusion | flops 134217728 | bytes 3667968 | tf_op jit(solution)/shard_map/conv_general_dilated | solution.py:20
  158.1 23.1 %all-gather.2.cloned.1.call-done = bf16[1024,8192]{1,0:T(8,128)(2,1)} async-done(((bf16[1024,512]{1,0:T(8,128)(2,1)}), bf16[1024,8192]{1,0:T(8,128)(2,1)}) %all-gather.2.cloned.1.call-update) | async-done | bytes 16777232 | tf_op jit(solution)/shard_map/all_gather | solution.py:81
  181.2 16.8 %multiply_bitcast_fusion = (f32[1,512,1024]{2,1,0:T(8,128)}, bf16[512,1024]{1,0:T(8,128)(2,1)S(1)}) fusion(f32[1,512,1024]{2,0,1:T(1,128)} %fusion.19, f32[1024]{0:T(1024)S(1)} %copy-done.20, bf16[504,1024]{1,0:T(8,128)(2,1)S(1)} %copy-done.7, bf16[8,1024]{1,0:T(8,128)(2,1)S(1)} %fusion.27, f32[3,504,1024]{2,1,0:T(8,128)} %copy-done.2, ...), kind=kOutput, calls=%fused_computation.39 | convolution fusion | flops 8595177472 | bytes 37752832 | tf_op jit(solution)/shard_map/dot_general | solution.py:90
  198.0 28.3 %fusion.15 = bf16[1,128,1024]{2,0,1:T(2,128)(2,1)S(1)} fusion(bf16[512,1,1024]{2,0,1:T(8,128)(2,1)S(1)} %bitcast.80, bf16[1,639,1024]{2,1,0:T(8,128)(2,1)} %copy-done.8), kind=kOutput, calls=%fused_computation.34 | convolution fusion | flops 134217728 | bytes 2619392 | tf_op jit(solution)/shard_map/conv_general_dilated | solution.py:20
  226.4 2.6 rev.23
  229.0 17.8 %convolution_convert_fusion = bf16[512,8192]{1,0:T(8,128)(2,1)} fusion(bf16[1024,8192]{1,0:T(8,128)(2,1)} %all-gather.2.cloned.1.call-done, f32[1,512,1024]{2,0,1:T(1,128)} %fusion.19, f32[1024]{0:T(1024)S(1)} %copy-done.20, bf16[504,1024]{1,0:T(8,128)(2,1)S(1)} %copy-done.7, bf16[8,1024]{1,0:T(8,128)(2,1)S(1)} %fusion.27, f32[3,504,1024]{2,1,0:T(8,128)} %copy-done.2, ...), kind=kOutput, calls=%fused_computation | convolution fusion | flops 8598847488 | bytes 34607104 | tf_op jit(solution)/shard_map/dot_general | solution.py:85
  246.9 2.4 broadcast_multiply_fusion
  249.3 7.8 %all-to-all-start.2 = ((bf16[16,128,1024]{2,1,0:T(8,128)(2,1)}), bf16[16,128,1024]{2,1,0:T(8,128)(2,1)}, u32[]{:S(2)}, u32[]{:S(2)}) async-start(bf16[16,128,1024]{2,1,0:T(8,128)(2,1)} %broadcast_multiply_fusion), calls=%async_computation.3 | async-start | bytes 8388608 | tf_op jit(solution)/shard_map/all_to_all | solution.py:98
  258.9 1.3 rev.21
  260.3 58.0 %all-to-all-done.2 = bf16[16,128,1024]{2,1,0:T(8,128)(2,1)} async-done(((bf16[16,128,1024]{2,1,0:T(8,128)(2,1)}), bf16[16,128,1024]{2,1,0:T(8,128)(2,1)}, u32[]{:S(2)}, u32[]{:S(2)}) %all-to-all-start.2) | async-done | bytes 4194336 | tf_op jit(solution)/shard_map/all_to_all | solution.py:98
  318.2 1.6 select_bitcast_fusion
  320.5 31.7 %fusion.4 = f32[1,512,1024]{2,0,1:T(1,128)S(1)} fusion(bf16[1,639,1024]{2,1,0:T(8,128)(2,1)S(1)} %fusion.21, bf16[128,1,1024]{2,0,1:T(8,128)(2,1)S(1)} %bitcast.83), kind=kOutput, calls=%fused_computation.20 | convolution fusion | flops 134217728 | bytes 3667968 | tf_op jit(solution)/shard_map/conv_general_dilated | solution.py:20
  352.7 10.3 %rev.22 = f32[512,1024]{1,0:T(8,128)} reverse(f32[512,1024]{1,0:T(8,128)S(1)} %bitcast.79), dimensions={0} | reverse | bytes 4194304 | tf_op jit(solution)/shard_map/jit(_flip)/rev | solution.py:103
  363.0 3.9 fusion.9
  367.0 0.9 pad_maximum_fusion.1
  367.9 0.7 copy-done.3
  368.7 1.1 multiply_convert_fusion.2
  369.8 4.0 all-to-all-start.3
  373.8 1.8 convert_multiply_fusion
  375.6 10.8 %all-to-all-done.3 = bf16[16,3,8,1024]{3,2,1,0:T(8,128)(2,1)S(1)} async-done(((bf16[16,3,8,1024]{3,2,1,0:T(8,128)(2,1)}), bf16[16,3,8,1024]{3,2,1,0:T(8,128)(2,1)S(1)}, u32[]{:S(2)}, u32[]{:S(2)}) %all-to-all-start.3) | async-done | bytes 786464 | tf_op jit(solution)/shard_map/all_to_all | solution.py:107
  386.4 0.6 select_bitcast_fusion.2
  387.1 2.8 pad_maximum_fusion
  390.4 0.7 copy-done.4
  391.1 0.7 copy-done.6
  391.8 5.6 %multiply_reduce_fusion.1 = (bf16[3,1024]{1,0:T(4,128)(2,1)S(1)}, bf16[3,1024]{1,0:T(4,128)(2,1)S(1)}, bf16[3,1024]{1,0:T(4,128)(2,1)S(1)}, bf16[3,512,1024]{2,1,0:T(8,128)(2,1)}) fusion(bf16[3,8,1024]{2,1,0:T(8,128)(2,1)S(1)} %copy-done.10, bf16[3,512,1024]{2,1,0:T(8,128)(2,1)S(1)} %copy-done.1, f32[1,512,1024]{2,1,0:T(8,128)S(1)} %copy-done.4, ...), kind=kLoop, calls=%fused_computation.11 | loop fusion | flops 36166656 | bytes 25270272 | tf_op jit(solution)/shard_map/reduce_sum | solution.py:120
  397.4 21.6 %all_gather.8 = bf16[16,3,3,1024]{3,2,1,0:T(4,128)(2,1)S(1)} all-gather(bf16[1,3,3,1024]{3,2,1,0:T(4,128)(2,1)S(1)} %copy.33), channel_id=1, replica_groups=mesh['ctx'=16,'tp'=8] {'ctx'}, dimensions={0}, use_global_device_ids=true | all-gather | bytes 313344 | tf_op jit(solution)/shard_map/all_gather | solution.py:134
  419.2 0.6 convert_multiply_fusion.1
  (62 shorter events, 2.6 us)
Async XLA Ops:
  7.2 14.7 %copy-start = (bf16[3,512,1024]{2,1,0:T(8,128)(2,1)S(1)}, bf16[3,512,1024]{2,1,0:T(8,128)(2,1)}, u32[]{:S(2)}) copy-start(bf16[3,512,1024]{2,1,0:T(8,128)(2,1)} %param.7) | copy-start | bytes 9437188
  7.2 14.5 %copy-start.19 = (f32[3,3,1024]{2,1,0:T(4,128)S(1)}, f32[3,3,1024]{2,1,0:T(4,128)}, u32[]{:S(2)}) copy-start(f32[3,3,1024]{2,1,0:T(4,128)} %param.8) | copy-start | bytes 110596
  7.2 174.1 %all-gather.2.cloned.1.call-start = ((), (), s32[]{:S(2)}) async-start(), calls=%async_computation.5 | async-start | bytes 17825792 | tf_op jit(solution)/shard_map/all_gather | solution.py:81
  13.8 28.0 %all-to-all-start = ((bf16[16,3,8,1024]{3,2,1,0:T(8,128)(2,1)}), bf16[16,3,8,1024]{3,2,1,0:T(8,128)(2,1)}, u32[]{:S(2)}, u32[]{:S(2)}) async-start(bf16[16,3,8,1024]{3,2,1,0:T(8,128)(2,1)} %broadcast_multiply_fusion.2), calls=%async_computation | async-start | bytes 1572864 | tf_op jit(solution)/shard_map/all_to_all | solution.py:67
  21.8 33.6 %copy-start.13 = (f32[3,1,1024]{2,0,1:T(4,128)}, f32[3,1,1024]{2,0,1:T(4,128)S(1)}, u32[]{:S(2)}) copy-start(f32[3,1,1024]{2,0,1:T(4,128)S(1)} %copy.65) | copy-start | bytes 36868
  21.8 33.5 %copy-start.15 = (f32[3,1024]{1,0:T(4,128)}, f32[3,1024]{1,0:T(4,128)S(1)}, u32[]{:S(2)}) copy-start(f32[3,1024]{1,0:T(4,128)S(1)} %get-tuple-element.17) | copy-start | bytes 36868
  21.8 33.5 %copy-start.17 = (f32[3,1024]{1,0:T(4,128)}, f32[3,1024]{1,0:T(4,128)S(1)}, u32[]{:S(2)}) copy-start(f32[3,1024]{1,0:T(4,128)S(1)} %get-tuple-element.18) | copy-start | bytes 36868
  24.1 2.7 copy-start.2
  29.4 16.9 %copy-start.21 = (s32[16]{0:T(128)S(1)}, s32[16]{0:T(128)}, u32[]{:S(2)}) copy-start(s32[16]{0:T(128)} %param.13) | copy-start | bytes 196
  29.4 18.8 %copy-start.11 = (bf16[128,1024]{1,0:T(8,128)(2,1)S(1)}, bf16[128,1024]{1,0:T(8,128)(2,1)}, u32[]{:S(2)}) copy-start(bf16[128,1024]{1,0:T(8,128)(2,1)} %param.9) | copy-start | bytes 786436
  41.7 80.4 %all-to-all-start.1 = ((bf16[16,128,1024]{2,1,0:T(8,128)(2,1)}), bf16[16,128,1024]{2,1,0:T(8,128)(2,1)}, u32[]{:S(2)}, u32[]{:S(2)}) async-start(bf16[16,128,1024]{2,1,0:T(8,128)(2,1)} %broadcast_multiply_fusion.1), calls=%async_computation.1 | async-start | bytes 8388608 | tf_op jit(solution)/shard_map/all_to_all | solution.py:68
  46.3 327.5 %all-reduce.2.cloned.1.call-start = ((), (), s32[]{:S(2)}) async-start(), calls=%async_computation.7 | async-start | bytes 524288 | tf_op jit(solution)/shard_map/psum | solution.py:133
  55.4 0.6 copy-start.9
  55.4 70.4 %copy-start.12 = (bf16[128,1024]{1,0:T(8,128)(2,1)S(1)}, bf16[128,1024]{1,0:T(8,128)(2,1)}, u32[]{:S(2)}) copy-start(bf16[128,1024]{1,0:T(8,128)(2,1)} %rev.19) | copy-start | bytes 786436
  124.7 1.1 copy-start.8
  125.8 55.4 %copy-start.7 = (bf16[504,1024]{1,0:T(8,128)(2,1)S(1)}, bf16[504,1024]{1,0:T(8,128)(2,1)}, u32[]{:S(2)}) copy-start(bf16[504,1024]{1,0:T(8,128)(2,1)} %fusion.36) | copy-start | bytes 3096580
  125.8 55.4 %copy-start.20 = (f32[1024]{0:T(1024)S(1)}, f32[1024]{0:T(1024)}, u32[]{:S(2)}) copy-start(f32[1024]{0:T(1024)} %param.10) | copy-start | bytes 12292
  229.0 190.8 %reduce-scatter.2.cloned.1.call-start = ((), (), s32[]{:S(2)}) async-start(), calls=%async_computation.6 | async-start | bytes 9437184 | tf_op jit(solution)/shard_map/reduce_scatter | solution.py:84
  249.3 69.0 %all-to-all-start.2 = ((bf16[16,128,1024]{2,1,0:T(8,128)(2,1)}), bf16[16,128,1024]{2,1,0:T(8,128)(2,1)}, u32[]{:S(2)}, u32[]{:S(2)}) async-start(bf16[16,128,1024]{2,1,0:T(8,128)(2,1)} %broadcast_multiply_fusion), calls=%async_computation.3 | async-start | bytes 8388608 | tf_op jit(solution)/shard_map/all_to_all | solution.py:98
  363.0 4.0 copy-start.5
  367.0 1.7 copy-start.3
  369.8 16.6 %all-to-all-start.3 = ((bf16[16,3,8,1024]{3,2,1,0:T(8,128)(2,1)}), bf16[16,3,8,1024]{3,2,1,0:T(8,128)(2,1)S(1)}, u32[]{:S(2)}, u32[]{:S(2)}) async-start(bf16[16,3,8,1024]{3,2,1,0:T(8,128)(2,1)} %multiply_convert_fusion.2), calls=%async_computation.4 | async-start | bytes 1572864 | tf_op jit(solution)/shard_map/all_to_all | solution.py:107
  387.1 3.3 copy-start.1
  387.1 4.0 copy-start.4
  387.1 4.7 %copy-start.6 = (f32[1,512,1024]{2,1,0:T(8,128)S(1)}, f32[1,512,1024]{2,1,0:T(8,128)}, u32[]{:S(2)}) copy-start(f32[1,512,1024]{2,1,0:T(8,128)} %get-tuple-element.12) | copy-start | bytes 6291460
  387.1 4.6 %copy-start.10 = (bf16[3,8,1024]{2,1,0:T(8,128)(2,1)S(1)}, bf16[3,8,1024]{2,1,0:T(8,128)(2,1)}, u32[]{:S(2)}) copy-start(bf16[3,8,1024]{2,1,0:T(8,128)(2,1)} %copy-done.9) | copy-start | bytes 147460
  387.1 4.6 %copy-start.14 = (f32[3,1,1024]{2,0,1:T(4,128)S(1)}, f32[3,1,1024]{2,0,1:T(4,128)}, u32[]{:S(2)}) copy-start(f32[3,1,1024]{2,0,1:T(4,128)} %copy-done.13) | copy-start | bytes 36868
  387.1 4.6 %copy-start.16 = (f32[3,1024]{1,0:T(4,128)S(1)}, f32[3,1024]{1,0:T(4,128)}, u32[]{:S(2)}) copy-start(f32[3,1024]{1,0:T(4,128)} %copy-done.15) | copy-start | bytes 36868
  387.1 4.6 %copy-start.18 = (f32[3,1024]{1,0:T(4,128)S(1)}, f32[3,1024]{1,0:T(4,128)}, u32[]{:S(2)}) copy-start(f32[3,1024]{1,0:T(4,128)} %copy-done.17) | copy-start | bytes 36868
Sparse Core Ops, SparseCore 0:
  10.1 171.0 all-gather.1
  229.1 118.2 all-reduce.1
  350.4 49.8 reduce-scatter.1
